TPU v7x, 1024 devices: a whole 8x8x8 slice. The times are simulated.
1024 devices in a mesh: dp: 16 (over z, core), ctx: 64 (over x, y).
Axes of the slice: x: 8, y: 8, z: 8, core: 2. Of those that a mesh axis runs over, the one named last changes fastest.
Arguments:
- tokens: bfloat16 [12288, 4096], P('ctx'), may hold values from -6 to 6
- w_in: bfloat16 [4096, 3, 4096], P('ctx', None, 'dp'), may hold values from -0.09375 to 0.09375
- short_filter: float32 [3, 3, 4096], P(None, None, 'dp'), may hold values from -3.5 to 3.5
- mode_decay: float32 [8, 4096], P(None, 'dp'), may hold values from 0 to 1
- residue: float32 [8, 4096], P(None, 'dp'), may hold values from -2 to 2
- w_out: bfloat16 [4096, 4096], P('dp'), may hold values from -0.125 to 0.125
Outputs:
- block_out: bfloat16 [12288, 4096], P('ctx', 'dp')
All inputs are finite; a program needn't handle non-finite values.
Results may differ from a plain program's by a relative error of at most 0.018.
Values may be sent and summed in bfloat16 or wider, within the bound.
A program may use at most 64 MiB of HBM per device.

v0:
```python
import jax
import jax.numpy as jnp
from jax import lax
from jax.sharding import PartitionSpec as P

BLK = 64


def from_behind(block, axis, distance):
    devices = range(lax.axis_size(axis))
    route = [(i - distance, i) for i in devices if i - distance in devices]
    return lax.ppermute(block, axis, route)


def from_everyone(array, axis):
    length = lax.axis_size(axis)
    return lax.all_to_all(
        jnp.broadcast_to(array[None], (length, *array.shape)), axis, 0, 0, tiled=True
    )


def joined_along(tiles, dim):
    tiles = jnp.moveaxis(tiles, 0, dim)
    dims = tiles.shape
    return tiles.reshape(*dims[:dim], dims[dim] * dims[dim + 1], *dims[dim + 2 :])


def gathered_copies(array, axis, dim):
    tiles = from_everyone(array, axis)
    return joined_along(tiles, dim)


def cut_along(array, dim, length):
    before, after = (array.shape[:dim], array.shape[dim + 1 :])
    return jnp.moveaxis(array.reshape(*before, length, -1, *after), dim, 0)


def summed_on_arrival(array, axis, dim):
    length = lax.axis_size(axis)
    tiles = lax.all_to_all(cut_along(array, dim, length), axis, 0, 0, tiled=True)
    return jnp.sum(tiles.astype(jnp.float32), axis=0)


def on_device(tokens, w_in, short_filter, mode_decay, residue, w_out):
    row_count = tokens.shape[0]
    chan_count = w_in.shape[2]
    short_count = short_filter.shape[0]
    mode_count = mode_decay.shape[0]
    earlier_rows = from_behind(tokens[row_count - (short_count - 1) :], "ctx", 1)
    source = jnp.concatenate([earlier_rows, tokens], 0)
    projected = jnp.einsum(
        "td,dgc->tgc",
        source,
        lax.all_gather(w_in, "ctx", axis=0, tiled=True),
        preferred_element_type=jnp.float32,
    )
    featured = jnp.zeros((row_count, 3, chan_count), jnp.float32)
    for j in range(short_count):
        featured = (
            featured
            + short_filter[j] * projected[short_count - 1 - j : short_count - 1 - j + row_count]
        )
    mixed = (featured[:, 1] * featured[:, 2]).astype(jnp.bfloat16)
    medium = mixed.astype(jnp.float32)
    highest = lax.Precision.HIGHEST
    mode_gain = residue * jnp.sqrt(1.0 - mode_decay * mode_decay)
    block_len = BLK
    block_times = jnp.arange(block_len).astype(jnp.float32)
    power_in = jnp.power(mode_decay[None], block_times[:, None, None])
    kernel_head = jnp.sum(mode_gain[None] * power_in, 1)
    lag_index = jnp.arange(block_len)[:, None] - jnp.arange(block_len)[None, :]
    toeplitz = jnp.where(
        (lag_index >= 0)[:, :, None], kernel_head[jnp.clip(lag_index, 0, block_len - 1)], 0.0
    )
    carry_weights = mode_gain[None] * power_in * mode_decay[None]
    state_weights = power_in[::-1]
    decay_block = jnp.power(mode_decay, float(block_len))
    blocks = medium.reshape(row_count // block_len, block_len, chan_count)

    def block_step(carried, block_rows):
        inner = jnp.einsum("tsc,sc->tc", toeplitz, block_rows, precision=highest)
        inner = inner + jnp.einsum("tnc,nc->tc", carry_weights, carried, precision=highest)
        carried = decay_block * carried + jnp.einsum(
            "snc,sc->nc", state_weights, block_rows, precision=highest
        )
        return (carried, inner)

    zero_state = jnp.zeros((mode_count, chan_count), jnp.float32)
    local_end, local_part = lax.scan(block_step, zero_state, blocks)
    local_part = local_part.reshape(row_count, chan_count)
    decay_device = jnp.power(mode_decay, float(row_count))
    own_index = lax.axis_index("ctx")
    shard_piece = gathered_copies(local_end[None], "ctx", 0)
    owners = jnp.arange(shard_piece.shape[0], dtype=jnp.int32)
    distance = own_index - 1 - owners
    factor = jnp.power(
        decay_device[None], jnp.maximum(distance, 0).astype(jnp.float32)[:, None, None]
    )
    factor = jnp.where((distance >= 0)[:, None, None], factor, 0.0)
    entering = jnp.sum(factor * shard_piece, 0)
    row_times = jnp.arange(1, row_count + 1).astype(jnp.float32)
    entry_weights = mode_gain[None] * jnp.power(mode_decay[None], row_times[:, None, None])
    long_part = local_part + jnp.einsum("tnc,nc->tc", entry_weights, entering, precision=highest)
    gated = (featured[:, 0] * long_part).astype(jnp.bfloat16)
    summed = summed_on_arrival(
        jnp.einsum("tc,cd->dt", gated, w_out, preferred_element_type=jnp.float32).astype(
            jnp.bfloat16
        ),
        "dp",
        0,
    )
    return summed.T.astype(jnp.bfloat16)


def solution(mesh):
    return jax.shard_map(
        on_device,
        mesh=mesh,
        in_specs=(
            P("ctx", None),
            P("ctx", None, "dp"),
            P(None, None, "dp"),
            P(None, "dp"),
            P(None, "dp"),
            P("dp", None),
        ),
        out_specs=P("ctx", "dp"),
        check_vma=False,
    )
```

profile of v0, /device:TPU:1, one launch (start us, length us, event | category | flops | bytes accessed | tf_op | source)
XLA Modules:
  0.0 227.5 jit_solution(4395317295688084976)
XLA Ops:
  6.5 0.0 copy-start
  6.5 0.0 all-gather.2.cloned.1.call-start
  6.5 0.7 all-gather.2.cloned.1.call-update
  7.3 0.9 slice.31
  8.1 4.1 %collective-permute-start = (bf16[2,4096]{1,0:T(2,128)(2,1)S(1)}, bf16[2,4096]{1,0:T(2,128)(2,1)S(1)}, u32[]{:S(2)}, u32[]{:S(2)}) collective-permute-start(bf16[2,4096]{1,0:T(2,128)(2,1)S(1)} %slice.31), channel_id=1, source_target_pairs={{0,1},{1,2},{2,3},{3,4},{4,5},{5,6},{6,7},{7,8},{8,9},{9,10},{10,1... | collective-permute-start | bytes 49160 | tf_op jit(solution)/shard_map/ppermute | solution.py:12
  12.3 0.1 reshape.84
  12.4 0.7 broadcast_power_fusion.1
  13.1 1.5 multiply_reduce_fusion.4
  14.6 16.1 %gather_fusion = f32[4096,256]{1,0:T(8,128)} fusion(f32[64,256]{1,0:T(8,128)S(1)} %get-tuple-element.113, s32[4096]{0:T(1024)S(1)} %broadcast_clamp_fusion), kind=kCustom, calls=%fused_computation | custom fusion | bytes 8404992 | tf_op jit(solution)/shard_map/gather | solution.py:73
  30.7 0.0 copy-start.3
  30.7 4.0 %broadcast_select_fusion = f32[64,64,256]{2,1,0:T(8,128)} fusion(f32[64,64,256]{2,1,0:T(8,128)} %bitcast.74, pred[64,64]{1,0:T(8,128)(4,1)S(1)} %subtract_compare_fusion), kind=kLoop, calls=%fused_computation.10 | loop fusion | flops 1048576 | bytes 8392704 | tf_op jit(solution)/shard_map/jit(_where)/select_n | solution.py:72
  34.7 0.0 copy-done.3
  34.7 0.0 collective-permute-done
  34.7 83.0 %all-gather.2.cloned.1.call-done = bf16[4096,3,256]{2,0,1:T(8,128)(2,1)} async-done(((bf16[64,3,256]{2,0,1:T(8,128)(2,1)}), bf16[4096,3,256]{2,0,1:T(8,128)(2,1)}) %all-gather.2.cloned.1.call-update) | async-done | bytes 6291472 | tf_op jit(solution)/shard_map/all_gather | solution.py:54
  117.7 4.7 %fusion.2 = f32[194,3,256]{2,0,1:T(8,128)S(1)} fusion(bf16[4096,3,256]{2,0,1:T(8,128)(2,1)} %all-gather.2.cloned.1.call-done, bf16[192,4096]{1,0:T(8,128)(2,1)} %param.8, bf16[2,4096]{1,0:T(2,128)(2,1)S(1)} %collective-permute-done), kind=kOutput, calls=%fused_computation.12 | convolution fusion | flops 1223720960 | bytes 8476672 | tf_op jit(solution)/shard_map/td,dgc->tgc/dot_general | solution.py:51
  122.5 0.0 copy-start.2
  122.5 0.2 fusion.5
  122.7 0.4 copy-done.2
  123.2 13.2 %while.13 = (s32[]{:T(128)}, f32[8,256]{1,0:T(8,128)S(1)}, f32[3,64,256]{2,1,0:T(8,128)}, f32[8,256]{1,0:T(8,128)S(1)}, f32[3,64,256]{2,1,0:T(8,128)S(1)}, /*ind...) while((s32[]{:T(128)}, f32[8,256]{1,0:T(8,128)S(1)}, ...), condition=%wide.region_2.3_spmd.clone, body=%wide.region_1.2_spmd.clone.sunk | while | flops 2871299 | bytes 5383043 | solution.py:89
  123.2 0.1 multiply_reduce_fusion.8
  123.3 0.8 multiply_reduce_fusion.10
  124.1 2.8 %multiply_reduce_fusion.9 = f32[256,64]{0,1:T(8,128)S(1)} fusion(f32[64,64,256]{2,1,0:T(8,128)} %get-tuple-element.213, f32[256,64]{0,1:T(8,128)S(1)} %dynamic-slice_bitcast_fusion.2), kind=kLoop, calls=%fused_computation.2.clone.1 | loop fusion | flops 2080768 | bytes 4325376 | tf_op jit(solution)/shard_map/while/body/eval_jaxpr/tsc,sc->tc/dot_general | solution.py:81
  126.9 0.6 bitcast_dynamic-update-slice_fusion.2
  127.6 0.1 multiply_reduce_fusion.8
  127.7 0.8 multiply_reduce_fusion.10
  128.5 2.8 %multiply_reduce_fusion.9 = f32[256,64]{0,1:T(8,128)S(1)} fusion(f32[64,64,256]{2,1,0:T(8,128)} %get-tuple-element.213, f32[256,64]{0,1:T(8,128)S(1)} %dynamic-slice_bitcast_fusion.2), kind=kLoop, calls=%fused_computation.2.clone.1 | loop fusion | flops 2080768 | bytes 4325376 | tf_op jit(solution)/shard_map/while/body/eval_jaxpr/tsc,sc->tc/dot_general | solution.py:81
  131.3 0.6 bitcast_dynamic-update-slice_fusion.2
  132.0 0.1 multiply_reduce_fusion.8
  132.1 0.8 multiply_reduce_fusion.10
  132.9 2.8 %multiply_reduce_fusion.9 = f32[256,64]{0,1:T(8,128)S(1)} fusion(f32[64,64,256]{2,1,0:T(8,128)} %get-tuple-element.213, f32[256,64]{0,1:T(8,128)S(1)} %dynamic-slice_bitcast_fusion.2), kind=kLoop, calls=%fused_computation.2.clone.1 | loop fusion | flops 2080768 | bytes 4325376 | tf_op jit(solution)/shard_map/while/body/eval_jaxpr/tsc,sc->tc/dot_general | solution.py:81
  135.7 0.6 bitcast_dynamic-update-slice_fusion.2
  136.4 0.0 copy-start.1
  136.4 0.8 broadcast_in_dim.60
  137.2 9.6 %all-to-all-start = ((f32[64,1,8,256]{3,2,1,0:T(8,128)}), f32[64,1,8,256]{3,2,1,0:T(8,128)S(1)}, u32[]{:S(2)}, u32[]{:S(2)}) async-start(f32[64,1,8,256]{3,2,1,0:T(8,128)} %broadcast_in_dim.60), calls=%async_computation | async-start | bytes 1048576 | tf_op jit(solution)/shard_map/all_to_all | solution.py:17
  146.8 16.3 %all-to-all-done = f32[64,1,8,256]{3,2,1,0:T(8,128)S(1)} async-done(((f32[64,1,8,256]{3,2,1,0:T(8,128)}), f32[64,1,8,256]{3,2,1,0:T(8,128)S(1)}, u32[]{:S(2)}, u32[]{:S(2)}) %all-to-all-start) | async-done | bytes 524320 | tf_op jit(solution)/shard_map/all_to_all | solution.py:17
  163.1 0.7 fusion.7
  163.8 2.2 multiply_reduce_fusion.3
  166.0 0.0 copy-done.1
  166.0 0.0 copy-done
  166.0 0.6 convolution_convert_fusion
  166.6 0.1 copy.38
  166.8 51.6 %all_to_all.10 = bf16[16,256,192]{1,2,0:T(8,128)(2,1)} all-to-all(bf16[16,256,192]{1,2,0:T(8,128)(2,1)S(1)} %bitcast.76), channel_id=1, replica_groups=mesh['dp'=16,'ctx'=64] {'dp'}, dimensions={0} | all-to-all | bytes 3145728 | tf_op jit(solution)/shard_map/all_to_all | solution.py:40
  218.4 2.3 %reduce_sum.32 = bf16[256,192]{0,1:T(8,128)(2,1)} reduce(bf16[16,256,192]{1,2,0:T(8,128)(2,1)} %all_to_all.10, bf16[]{:T(256)} %constant.16.clone.1), dimensions={0}, to_apply=%region_4.5 | reduce | flops 737280 | bytes 1671170 | tf_op jit(solution)/shard_map/reduce_sum | solution.py:41
  (20 shorter events, 0.2 us)
Async XLA Ops:
  6.5 159.5 %copy-start = (bf16[256,4096]{1,0:T(8,128)(2,1)S(1)}, bf16[256,4096]{1,0:T(8,128)(2,1)}, u32[]{:S(2)}) copy-start(bf16[256,4096]{1,0:T(8,128)(2,1)} %param.13) | copy-start | bytes 6291460
  6.5 111.2 %all-gather.2.cloned.1.call-start = ((), (), s32[]{:S(2)}) async-start(), calls=%async_computation.2 | async-start | bytes 6389760 | tf_op jit(solution)/shard_map/all_gather | solution.py:54
  8.1 26.6 %collective-permute-start = (bf16[2,4096]{1,0:T(2,128)(2,1)S(1)}, bf16[2,4096]{1,0:T(2,128)(2,1)S(1)}, u32[]{:S(2)}, u32[]{:S(2)}) collective-permute-start(bf16[2,4096]{1,0:T(2,128)(2,1)S(1)} %slice.31), channel_id=1, source_target_pairs={{0,1},{1,2},{2,3},{3,4},{4,5},{5,6},{6,7},{7,8},{8,9},{9,10},{10,1... | collective-permute-start | bytes 49160 | tf_op jit(solution)/shard_map/ppermute | solution.py:12
  30.7 4.0 %copy-start.3 = (f32[3,3,256]{2,1,0:T(4,128)S(1)}, f32[3,3,256]{2,1,0:T(4,128)}, u32[]{:S(2)}) copy-start(f32[3,3,256]{2,1,0:T(4,128)} %param.10) | copy-start | bytes 27652
  122.5 0.7 copy-start.2
  136.4 29.6 %copy-start.1 = (f32[3,64,256]{2,1,0:T(8,128)S(1)}, f32[3,64,256]{2,1,0:T(8,128)}, u32[]{:S(2)}) copy-start(f32[3,64,256]{2,1,0:T(8,128)} %get-tuple-element.48) | copy-start | bytes 589828
  137.2 25.9 %all-to-all-start = ((f32[64,1,8,256]{3,2,1,0:T(8,128)}), f32[64,1,8,256]{3,2,1,0:T(8,128)S(1)}, u32[]{:S(2)}, u32[]{:S(2)}) async-start(f32[64,1,8,256]{3,2,1,0:T(8,128)} %broadcast_in_dim.60), calls=%async_computation | async-start | bytes 1048576 | tf_op jit(solution)/shard_map/all_to_all | solution.py:17
Sparse Core Ops, SparseCore 0:
  11.6 106.1 all-gather.1
where the time goes:
time: 228 us
  waiting for transfers between devices  100 us (44%)
  blocking collectives  51.6 us (23%)
  other arithmetic  24.8 us (11%)
  local copies, waits for them, and re-layouts  18.5 us (8%)
  starting transfers between devices  13.7 us (6%)
  between operations  13.6 us (6%)
  matrix products  5.31 us (2%)
    all_gather x1, waiting for transfers between devices, on_device(): lax.all_gather(w_in, 'ctx', axis=0, tiled=True)  83 us
    all_to_all x1, blocking collectives, summed_on_arrival(): lax.all_to_all(cut_along(array, dim, length), axis, 0, 0, tiled=True)  51.6 us
    all_to_all x1, waiting for transfers between devices, from_everyone(): lax.all_to_all(jnp.broadcast_to(array[None], (length, *array.shape)), axi...  16.3 us
    gather x1, local copies, waits for them, and re-layouts, on_device(): kernel_head[jnp.clip(lag_index, 0, block_len - 1)]  16.1 us
    all_to_all x1, starting transfers between devices, from_everyone(): lax.all_to_all(jnp.broadcast_to(array[None], (length, *array.shape)), axi...  9.57 us
    dot_general x3, other arithmetic, block_step(): inner = jnp.einsum('tsc,sc->tc', toeplitz, block_rows, precision=highest)  8.5 us
    dot_general x1, matrix products, on_device(): jnp.einsum('td,dgc->tgc', source, lax.all_gather(w_in, 'ctx', axis=0, til...  4.72 us
  transfers between devices with their start and end apart: 3, of which 2 were waited for; matrix products, arithmetic and copies ran while one was open for 10% of the time, Pallas kernels for 0%

commit v1 on v0

v1 whole, which is shorter than its diff:
```python
import functools
import heapq
import math

import jax
import jax.numpy as jnp
from jax import lax
from jax.experimental import pallas as pl
from jax.experimental.pallas import tpu as pltpu
from jax.sharding import PartitionSpec as P

MESH = pl.DeviceIdType.MESH
HALO = 16
CHUNKS = 8
SPANS = ((1, 3), (0, 1))


def offset_of(j):
    return (j + 1) // 2 * (1 if j % 2 else -1)


def arrival_plan(n):
    half = n // 2
    cost = (0.73, 0.365)
    delay = 1.7
    free = {1: 0.0, -1: 0.0}
    heap, order, seen = [], [], {}
    count = 0

    def send(now, item):
        nonlocal count
        kind, part, j, way, far = item
        length = cost[part] * (0.5 if kind == "u" and far == half else 1.0)
        free[way] = max(free[way], now) + length
        count += 1
        heapq.heappush(heap, (free[way] + delay, count, item))
        return item

    def spread(now, part, j):
        return [send(now, ("v", part, j, way, 1)) for way in (1, -1) if half > 1 or way == (1 if j % 2 == 0 else -1)]

    first = []
    for part in (0, 1):
        first += [send(0.0, ("u", part, 0, way, 1)) for way in (1, -1)]
        if part == 0:
            first += spread(0.0, 0, 0)
    left = n * (n - 1)
    sent_v = 2 if half > 1 else 1
    held = [0]
    while heap:
        now, _, item = heapq.heappop(heap)
        kind, part, j, way, far = item
        out = []
        if kind == "u":
            if far < half:
                out.append(send(now, ("u", part, 0, way, far + 1)))
                block = 2 * far - 1 if way == -1 else 2 * far
            else:
                seen[part] = seen.get(part, 0) + 1
                block = n - 1 if seen[part] == 2 else None
            if block is not None:
                if part == 0:
                    more = spread(now, 0, block)
                    sent_v += len(more)
                    out += more
                else:
                    held.append(block)
        else:
            limit = half if (j % 2 == 0) == (way == 1) else half - 1
            if far < limit:
                out.append(send(now, ("v", part, j, way, far + 1)))
                sent_v += part == 0
        if sent_v >= left and held and len(held) == n:
            for block in held:
                out += spread(now, 1, block)
            held = []
        order.append((now, item, out))
    return first, order


def kernel(n, zs, tok_hbm, ws_hbm, taps_ref, decay_ref, residue_ref, wo_hbm, out_ref,
           gathered, tokens, shuffled, halo, wout, acc, mixed, long, entry, line_y, line_x, gated,
           outgoing, incoming, local_sem, send_sem, recv_sem, wo_send, wo_recv, halo_sem,
           state_send, state_recv, swap_sem, rs_send, rs_recv):
    rows = tok_hbm.shape[0]
    chans = ws_hbm.shape[2]
    depth = ws_hbm.shape[1]
    half = n // 2
    wide = n * depth
    lanes = chans // 2
    steps = rows // CHUNKS
    modes = decay_ref.shape[0]
    dp = lax.axis_index("dp")
    ctx = lax.axis_index("ctx")
    core = lax.rem(dp, 2)
    z = dp // 2
    x = ctx // n
    y = lax.rem(ctx, n)
    swap = core == 1
    u = jnp.where(swap, x, y)
    v = jnp.where(swap, y, x)

    def at_uv(uu, vv):
        return {"dp": dp, "ctx": jnp.where(swap, uu * n + vv, vv * n + uu)}

    def at_xy(xx, yy):
        return {"dp": dp, "ctx": xx * n + yy}

    def at_z(zz):
        return {"dp": zz * 2 + core, "ctx": ctx}

    mate = {"dp": z * 2 + 1 - core, "ctx": ctx}
    after = {"dp": dp, "ctx": lax.rem(ctx + 1, n * n)}
    before = {"dp": dp, "ctx": lax.rem(ctx + n * n - 1, n * n)}

    def wrap(i, size):
        return lax.rem(i + size, size)

    peers = [at_xy(x, lax.rem(y + d, n)) for d in range(1, n)]
    peers += [at_xy(lax.rem(x + d, n), y) for d in range(1, n)]
    peers += [at_z(wrap(z + 1, zs)), at_z(wrap(z - 1, zs)), mate, after, before]
    barrier = pltpu.get_barrier_semaphore()
    for peer in peers:
        pl.semaphore_signal(barrier, inc=1, device_id=peer, device_id_type=MESH)

    own_copy = pltpu.make_async_copy(ws_hbm, gathered.at[:, v, u], local_sem.at[0])
    own_copy.start()
    tok_copy = pltpu.make_async_copy(tok_hbm, tokens, local_sem.at[1])
    tok_copy.start()
    wo_copies = []
    for t in range(zs):
        wo_copies.append(pltpu.make_async_copy(
            wo_hbm.at[:, pl.ds(pl.multiple_of((2 * t + core) * chans, 128), chans)],
            wout.at[t, core], local_sem.at[2 + t]))
        wo_copies[-1].start()

    first, order = arrival_plan(n)
    index = {}

    def transfer(item):
        kind, part, j, way, far = item
        lo, hi = SPANS[part]
        number = index.setdefault(item, len(index))
        if kind == "u":
            uu = wrap(u - way * (far - 1), n)
            ref = gathered.at[lo:hi, v, uu]
            src = ws_hbm.at[lo:hi] if far == 1 else ref
            if far == half:
                cut = slice(0, depth // 2) if way == 1 else slice(depth // 2, depth)
                src, ref = src.at[:, cut], ref.at[:, cut]
            target = at_uv(wrap(u + way, n), v)
        else:
            uu = wrap(u + offset_of(j), n)
            vv = wrap(v - way * (far - 1), n)
            ref = gathered.at[lo:hi, vv, uu]
            src = ws_hbm.at[lo:hi] if far == 1 and j == 0 else ref
            target = at_uv(u, wrap(v + way, n))
        return pltpu.make_async_remote_copy(
            src_ref=src, dst_ref=ref, send_sem=send_sem.at[number], recv_sem=recv_sem.at[number],
            device_id=target, device_id_type=MESH)

    pl.semaphore_wait(barrier, len(peers))
    sends = []

    def start(item):
        copy = transfer(item)
        copy.start()
        sends.append(copy)

    for item in first[:4]:
        start(item)
    halo_copy = pltpu.make_async_remote_copy(
        src_ref=tok_hbm.at[rows - 8:rows], dst_ref=halo, send_sem=halo_sem.at[0], recv_sem=halo_sem.at[1],
        device_id=after, device_id_type=MESH)
    halo_copy.start()
    for item in first[4:]:
        start(item)
    wo_remote = []
    for t in range(zs):
        wo_remote.append(pltpu.make_async_remote_copy(
            src_ref=wo_hbm.at[:, pl.ds(pl.multiple_of((2 * t + 1 - core) * chans, 128), chans)],
            dst_ref=wout.at[t, core], send_sem=wo_send.at[t], recv_sem=wo_recv.at[t],
            device_id=mate, device_id_type=MESH))
        wo_remote[-1].start()

    tok_copy.wait()
    lane = lax.broadcasted_iota(jnp.int32, (1, 128), 1)
    per = 128 // depth

    def rearranged(read, write):
        @pl.when(core == 0)
        def _():
            for b in range(n):
                write(b, 0, wide, read(b * wide, wide))

        @pl.when(core == 1)
        def _():
            for q in range(n // per):
                for t in range(n // per):
                    near = read(per * t * wide + q * 128, 128)
                    far = read((per * t + 1) * wide + q * 128, 128)
                    write(2 * q, t * 128, 128, jnp.where(lane < 64, near, pltpu.roll(far, 64, 1)))
                    write(2 * q + 1, t * 128, 128, jnp.where(lane < 64, pltpu.roll(near, 64, 1), far))

    def write_rows(b, col, size, value):
        shuffled[b, HALO:HALO + rows, col:col + size] = value.astype(jnp.bfloat16)

    def write_halo(b, col, size, value):
        value = jnp.where(ctx > 0, value, 0.0)
        shuffled[b, 0:HALO, col:col + size] = jnp.concatenate([jnp.zeros_like(value), value], 0).astype(jnp.bfloat16)

    rearranged(lambda col, size: tokens[:, col:col + size].astype(jnp.float32), write_rows)
    acc[...] = jnp.zeros_like(acc)
    own_copy.wait()
    halo_copy.wait()
    rearranged(lambda col, size: halo[:, col:col + size].astype(jnp.float32), write_halo)

    def multiply(g, vv):
        acc[g] += jnp.dot(shuffled[vv], gathered[g, vv].reshape(wide, chans), preferred_element_type=jnp.float32)

    def featured(g):
        value = acc[g]
        total = taps_ref[0, g:g + 1, :] * value[HALO:]
        for j in range(1, taps_ref.shape[0]):
            total = total + taps_ref[j, g:g + 1, :] * pltpu.roll(value, j, 0)[HALO:]
        return total

    decay = decay_ref[...]
    powers = {1: decay}

    def power(k):
        if k not in powers:
            low = k // 2
            powers[k] = power(low) * power(k - low)
        return powers[k]

    chunk = lax.broadcasted_iota(jnp.int32, (CHUNKS, lanes), 0)

    def row_of(value, m, h):
        return jnp.broadcast_to(value[m:m + 1, h * lanes:(h + 1) * lanes], (CHUNKS, lanes))

    state_copies = []

    def share(ref, mine, stage, target):
        for d in range(1, n):
            copy = pltpu.make_async_remote_copy(
                src_ref=ref.at[mine], dst_ref=ref.at[mine], send_sem=state_send.at[stage, d],
                recv_sem=state_recv.at[stage, d], device_id=target(d), device_id_type=MESH)
            copy.start()
            state_copies.append(copy)

    def received(stage):
        for copy in state_copies[stage * (n - 1):(stage + 1) * (n - 1)]:
            copy.wait_recv()

    def task_local():
        value = (featured(1) * featured(2)).astype(jnp.bfloat16).astype(jnp.float32)
        for h in range(2):
            mixed[h] = value[:, h * lanes:(h + 1) * lanes]
        for h in range(2):
            rates = [row_of(decay, m, h) for m in range(modes)]
            states = [jnp.zeros((CHUNKS, lanes), jnp.float32)] * modes
            for i in range(steps):
                fresh = mixed[h, pl.ds(i, CHUNKS, stride=steps), :]
                states = [r * s + fresh for r, s in zip(rates, states)]
            for m in range(modes):
                state = states[m]
                for k in (1, 2, 4):
                    moved = jnp.where(chunk >= k, pltpu.roll(state, k, 0), 0.0)
                    state = state + row_of(power(steps * k), m, h) * moved
                entry[m, h] = jnp.where(chunk >= 1, pltpu.roll(state, 1, 0), 0.0)
                line_y[y, m:m + 1, h * lanes:(h + 1) * lanes] = state[CHUNKS - 1:, :]
        share(line_y, y, 0, lambda d: at_xy(x, lax.rem(y + d, n)))

    def task_row():
        received(0)
        whole = power(rows)
        total = jnp.zeros_like(decay)
        for i in range(n):
            total = total * whole + line_y[i]
        line_x[x] = total
        share(line_x, x, 1, lambda d: at_xy(lax.rem(x + d, n), y))

    def task_long():
        received(1)
        whole = power(rows)
        line = power(rows * n)
        carried = jnp.zeros_like(decay)
        for i in range(n - 1):
            carried = jnp.where(i < x, carried * line + line_x[i], carried)
        for i in range(n - 1):
            carried = jnp.where(i < y, carried * whole + line_y[i], carried)
        gain = residue_ref[...] * jnp.sqrt(1.0 - decay * decay)
        for h in range(2):
            rates = [row_of(decay, m, h) for m in range(modes)]
            gains = [row_of(gain, m, h) for m in range(modes)]
            states = []
            for m in range(modes):
                reach = row_of(carried, m, h)
                for k in (1, 2, 4):
                    reach = jnp.where((chunk & k) != 0, reach * row_of(power(steps * k), m, h), reach)
                states.append(entry[m, h] + reach)
            for i in range(steps):
                fresh = mixed[h, pl.ds(i, CHUNKS, stride=steps), :]
                states = [r * s + fresh for r, s in zip(rates, states)]
                terms = [g * s for g, s in zip(gains, states)]
                while len(terms) > 1:
                    terms = [a + b for a, b in zip(terms[::2], terms[1::2])]
                long[h, pl.ds(i, CHUNKS, stride=steps), :] = terms[0]

    need = {}
    for item in [it for _, it, _ in order]:
        kind, part, j, way, far = item
        key = (part, 0) if kind == "u" else (part, (way * far) if far < half else half)
        need[key] = need.get(key, 0) + 1
    agenda = []
    done_first = 0.0
    pending = dict(need)
    for now, item, out in order:
        kind, part, j, way, far = item
        key = (part, 0) if kind == "u" else (part, (way * far) if far < half else half)
        pending[key] -= 1
        agenda.append((now, 0, len(agenda), "recv", item, out))
        if pending[key] == 0:
            agenda.append((now, 1, len(agenda), "dot", key, None))
            if part == 0:
                done_first = max(done_first, now)
    for wait, job in ((0.01, task_local), (6.5, task_row), (11.5, task_long)):
        agenda.append((done_first + wait, 2, len(agenda), "task", job, None))
    for _, _, _, what, item, out in sorted(agenda, key=lambda a: a[:3]):
        if what == "recv":
            transfer(item).wait_recv()
            for more in out:
                start(more)
        elif what == "dot":
            part, far = item
            for g in range(*SPANS[part]):
                multiply(g, wrap(v - far, n))
        else:
            item()

    for h in range(2):
        sel = slice(h * lanes, (h + 1) * lanes)
        value = acc[0][:, sel]
        total = taps_ref[0, 0:1, sel] * value[HALO:]
        for j in range(1, taps_ref.shape[0]):
            total = total + taps_ref[j, 0:1, sel] * pltpu.roll(value, j, 0)[HALO:]
        gated[core, :, sel] = (total * long[h]).astype(jnp.bfloat16)
    swap_copy = pltpu.make_async_remote_copy(
        src_ref=gated.at[core], dst_ref=gated.at[core], send_sem=swap_sem.at[0], recv_sem=swap_sem.at[1],
        device_id=mate, device_id_type=MESH)
    swap_copy.start()
    for copy in wo_copies:
        copy.wait()
    for copy in wo_remote:
        copy.wait_recv()
    swap_copy.wait_recv()

    def partial_of(distance):
        t = wrap(z + distance, zs)
        return (jnp.dot(gated[0], wout[t, 0], preferred_element_type=jnp.float32)
                + jnp.dot(gated[1], wout[t, 1], preferred_element_type=jnp.float32))

    far_z = zs // 2
    cut = rows // 2
    parts = {0: slice(0, cut), 1: slice(cut, rows)}
    rs_copies = {}

    def rs_copy(side, step, piece):
        way = 1 if side == 0 else -1
        copy = pltpu.make_async_remote_copy(
            src_ref=outgoing.at[side, step, parts[piece]], dst_ref=incoming.at[side, step, parts[piece]],
            send_sem=rs_send.at[side, step, piece], recv_sem=rs_recv.at[side, step, piece],
            device_id=at_z(wrap(z + way, zs)), device_id_type=MESH)
        rs_copies[side, step, piece] = copy
        return copy

    value = partial_of(far_z)
    for side in range(2):
        outgoing[side, 0, parts[side]] = value[parts[side]].astype(jnp.bfloat16)
        rs_copy(side, 0, side).start()
    for step in range(1, far_z):
        for side in range(2):
            way = 1 if side == 0 else -1
            value = partial_of(way * (far_z - step))
            for piece in (1 - side, side):
                have = value[parts[piece]]
                if step > 1 or piece == side:
                    rs_copies[side, step - 1, piece].wait_recv()
                    have = have + incoming[side, step - 1, parts[piece]].astype(jnp.float32)
                outgoing[side, step, parts[piece]] = have.astype(jnp.bfloat16)
                rs_copy(side, step, piece).start()
    value = partial_of(0)
    for piece in range(2):
        have = value[parts[piece]]
        for side in range(2):
            rs_copies[side, far_z - 1, piece].wait_recv()
            have = have + incoming[side, far_z - 1, parts[piece]].astype(jnp.float32)
        out_ref[parts[piece]] = have.astype(jnp.bfloat16)

    for copy in sends + wo_remote + state_copies + [swap_copy] + list(rs_copies.values()):
        copy.wait_send()


def on_device(n, zs, tokens, w_in, short_filter, mode_decay, residue, w_out):
    rows = tokens.shape[0]
    depth, streams, chans = w_in.shape
    modes = mode_decay.shape[0]
    lanes = chans // 2
    first, order = arrival_plan(n)
    moves = len(order)
    far_z = zs // 2
    hbm = pl.BlockSpec(memory_space=pltpu.HBM)
    vmem = pl.BlockSpec(memory_space=pltpu.VMEM)
    dma = pltpu.SemaphoreType.DMA
    f32, b16 = jnp.float32, jnp.bfloat16
    return pl.pallas_call(
        functools.partial(kernel, n, zs),
        out_shape=jax.ShapeDtypeStruct((rows, chans), b16),
        in_specs=[hbm, hbm, vmem, vmem, vmem, hbm],
        out_specs=vmem,
        scratch_shapes=[
            pltpu.VMEM((streams, n, n, depth, chans), b16),
            pltpu.VMEM((rows, n * n * depth), b16),
            pltpu.VMEM((n, HALO + rows, n * depth), b16),
            pltpu.VMEM((8, n * n * depth), b16),
            pltpu.VMEM((zs, 2, chans, chans), b16),
            pltpu.VMEM((streams, HALO + rows, chans), f32),
            pltpu.VMEM((2, rows, lanes), f32),
            pltpu.VMEM((2, rows, lanes), f32),
            pltpu.VMEM((modes, 2, CHUNKS, lanes), f32),
            pltpu.VMEM((n, modes, chans), f32),
            pltpu.VMEM((n, modes, chans), f32),
            pltpu.VMEM((2, rows, chans), b16),
            pltpu.VMEM((2, far_z, rows, chans), b16),
            pltpu.VMEM((2, far_z, rows, chans), b16),
            dma((2 + zs,)), dma((moves,)), dma((moves,)), dma((zs,)), dma((zs,)), dma((2,)),
            dma((2, n)), dma((2, n)), dma((2,)), dma((2, far_z, 2)), dma((2, far_z, 2)),
        ],
        compiler_params=pltpu.CompilerParams(
            collective_id=0, has_side_effects=True, vmem_limit_bytes=60 * 1024 * 1024),
    )(tokens, jnp.transpose(w_in, (1, 0, 2)), short_filter, mode_decay, residue, w_out)


def solution(mesh):
    n = math.isqrt(mesh.shape["ctx"])
    zs = mesh.shape["dp"] // 2
    return jax.shard_map(
        functools.partial(on_device, n, zs),
        mesh=mesh,
        in_specs=(
            P("ctx", None),
            P("ctx", None, "dp"),
            P(None, None, "dp"),
            P(None, "dp"),
            P(None, "dp"),
            P("dp", None),
        ),
        out_specs=P("ctx", "dp"),
        check_vma=False,
    )
```

time: 228 us -> 90.5 us (0.40)
  waiting for transfers between devices: 100 us -> 0 us
  Pallas kernels: 0 us -> 88.8 us
  blocking collectives: 51.6 us -> 0 us
  other arithmetic: 24.8 us -> 0 us
  local copies, waits for them, and re-layouts: 18.5 us -> 1.54 us
  starting transfers between devices: 13.7 us -> 0 us
  between operations: 13.6 us -> 0.01 us
  matrix products: 5.31 us -> 0 us
    pallas_call x0 -> x1, Pallas kernels: none -> 88.8 us  [on_device(): pl.pallas_call(functools.partial(kernel, n, zs), out_shape=jax.ShapeDtype...]
    all_gather x1 -> x0, waiting for transfers between devices: 83 us -> none  [on_device(): lax.all_gather(w_in, 'ctx', axis=0, tiled=True)]
    all_to_all x1 -> x0, blocking collectives: 51.6 us -> none  [summed_on_arrival(): lax.all_to_all(cut_along(array, dim, length), axis, 0, 0, tiled=True)]
    all_to_all x1 -> x0, waiting for transfers between devices: 16.3 us -> none  [from_everyone(): lax.all_to_all(jnp.broadcast_to(array[None], (length, *array.shape)), axi...]
    gather x1 -> x0, local copies, waits for them, and re-layouts: 16.1 us -> none  [on_device(): kernel_head[jnp.clip(lag_index, 0, block_len - 1)]]
    dot_general x10 -> x0, other arithmetic: 13.4 us -> none  [the longest x3 8.5 us: block_step(): inner = jnp.einsum('tsc,sc->tc', toeplitz, block_rows, precision=highest)]
    all_to_all x1 -> x0, starting transfers between devices: 9.57 us -> none  [from_everyone(): lax.all_to_all(jnp.broadcast_to(array[None], (length, *array.shape)), axi...]
    dot_general x2 -> x0, matrix products: 5.31 us -> none  [the longest x1 4.72 us: on_device(): jnp.einsum('td,dgc->tgc', source, lax.all_gather(w_in, 'ctx', axis=0, til...]
  transfers between devices with their start and end apart: 3 -> 0, of which waited for: 2 -> 0; matrix products, arithmetic and copies ran while one was open for 10% -> 0% of each run, Pallas kernels for 0% -> 0%
where the time goes in v1:
time: 90.5 us; the launch traced here: 90.3 us
  Pallas kernels  88.8 us (98%)
  local copies, waits for them, and re-layouts  1.54 us (2%)
    pallas_call x1, Pallas kernels, on_device(): pl.pallas_call(functools.partial(kernel, n, zs), out_shape=jax.ShapeDtype...  88.8 us

profile of v1, /device:TPU:1, one launch (start us, length us, event | category | flops | bytes accessed | tf_op | source)
XLA Modules:
  0.0 90.3 jit_solution(13995920522049500253)
XLA Ops:
  0.0 88.8 %shard_map.64 = bf16[192,256]{1,0:T(8,128)(2,1)} custom-call(bf16[192,4096]{1,0:T(8,128)(2,1)} %tok_hbm.1, bf16[3,64,256]{2,1,0:T(8,128)(2,1)} %bitcast.1, f32[3,3,256]{2,1,0:T(4,128)} %taps_ref.1, f32[8,256]{1,0:T(8,128)} %decay_ref.1, f32[8,256]{1,0:T(8,128)} %residue_ref.1, bf16[256,4096]{1,0:T(8,128)(2,1)} %wo_hbm.1), custom_call_target="tpu_custom_call" | custom-call | tf_op jit(solution)/shard_map/pallas_call | solution.py:417
  88.8 1.5 %copy.8 = bf16[192,256]{1,0:T(8,128)(2,1)} copy(bf16[192,256]{1,0:T(8,128)(2,1)} %shard_map.64) | data formatting | bytes 196608

commit v2 on v1

--- a/solution.py
+++ b/solution.py
@@ -12,6 +12,7 @@
 MESH = pl.DeviceIdType.MESH
 HALO = 16
 CHUNKS = 8
+PIECES = 4
 SPANS = ((1, 3), (0, 1))
 
 
@@ -81,7 +82,7 @@
 def kernel(n, zs, tok_hbm, ws_hbm, taps_ref, decay_ref, residue_ref, wo_hbm, out_ref,
            gathered, tokens, shuffled, halo, wout, acc, mixed, long, entry, line_y, line_x, gated,
            outgoing, incoming, local_sem, send_sem, recv_sem, wo_send, wo_recv, halo_sem,
-           state_send, state_recv, swap_sem, rs_send, rs_recv):
+           state_send, state_recv, swap_sem, rs_out, rs_in):
     rows = tok_hbm.shape[0]
     chans = ws_hbm.shape[2]
     depth = ws_hbm.shape[1]
@@ -114,10 +115,17 @@
     before = {"dp": dp, "ctx": lax.rem(ctx + n * n - 1, n * n)}
 
     def wrap(i, size):
-        return lax.rem(i + size, size)
-
-    peers = [at_xy(x, lax.rem(y + d, n)) for d in range(1, n)]
-    peers += [at_xy(lax.rem(x + d, n), y) for d in range(1, n)]
+        return jnp.where(i >= size, i - size, jnp.where(i < 0, i + size, i))
+
+    u_at = {d: wrap(u + d, n) for d in range(1 - n, n)}
+    v_at = {d: wrap(v + d, n) for d in range(1 - n, n)}
+    z_at = {d: wrap(z + d, zs) for d in range(1 - zs, zs)}
+    to_u = {d: at_uv(u_at[d], v) for d in u_at}
+    to_v = {d: at_uv(u, v_at[d]) for d in v_at}
+    to_z = {d: at_z(z_at[d]) for d in (1, -1)}
+
+    peers = [at_xy(x, wrap(y + d, n)) for d in (1, -1)]
+    peers += [at_xy(wrap(x + d, n), y) for d in (1, -1)]
     peers += [at_z(wrap(z + 1, zs)), at_z(wrap(z - 1, zs)), mate, after, before]
     barrier = pltpu.get_barrier_semaphore()
     for peer in peers:
@@ -142,19 +150,19 @@
         lo, hi = SPANS[part]
         number = index.setdefault(item, len(index))
         if kind == "u":
-            uu = wrap(u - way * (far - 1), n)
+            uu = u_at[-way * (far - 1)]
             ref = gathered.at[lo:hi, v, uu]
             src = ws_hbm.at[lo:hi] if far == 1 else ref
             if far == half:
                 cut = slice(0, depth // 2) if way == 1 else slice(depth // 2, depth)
                 src, ref = src.at[:, cut], ref.at[:, cut]
-            target = at_uv(wrap(u + way, n), v)
+            target = to_u[way]
         else:
-            uu = wrap(u + offset_of(j), n)
-            vv = wrap(v - way * (far - 1), n)
+            uu = u_at[offset_of(j)]
+            vv = v_at[-way * (far - 1)]
             ref = gathered.at[lo:hi, vv, uu]
             src = ws_hbm.at[lo:hi] if far == 1 and j == 0 else ref
-            target = at_uv(u, wrap(v + way, n))
+            target = to_v[way]
         return pltpu.make_async_remote_copy(
             src_ref=src, dst_ref=ref, send_sem=send_sem.at[number], recv_sem=recv_sem.at[number],
             device_id=target, device_id_type=MESH)
@@ -270,7 +278,7 @@
                     state = state + row_of(power(steps * k), m, h) * moved
                 entry[m, h] = jnp.where(chunk >= 1, pltpu.roll(state, 1, 0), 0.0)
                 line_y[y, m:m + 1, h * lanes:(h + 1) * lanes] = state[CHUNKS - 1:, :]
-        share(line_y, y, 0, lambda d: at_xy(x, lax.rem(y + d, n)))
+        share(line_y, y, 0, lambda d: at_xy(x, wrap(y + d, n)))
 
     def task_row():
         received(0)
@@ -279,7 +287,7 @@
         for i in range(n):
             total = total * whole + line_y[i]
         line_x[x] = total
-        share(line_x, x, 1, lambda d: at_xy(lax.rem(x + d, n), y))
+        share(line_x, x, 1, lambda d: at_xy(wrap(x + d, n), y))
 
     def task_long():
         received(1)
@@ -335,7 +343,7 @@
         elif what == "dot":
             part, far = item
             for g in range(*SPANS[part]):
-                multiply(g, wrap(v - far, n))
+                multiply(g, v_at[-far])
         else:
             item()
 
@@ -357,46 +365,50 @@
     swap_copy.wait_recv()
 
     def partial_of(distance):
-        t = wrap(z + distance, zs)
+        t = z_at[distance]
         return (jnp.dot(gated[0], wout[t, 0], preferred_element_type=jnp.float32)
                 + jnp.dot(gated[1], wout[t, 1], preferred_element_type=jnp.float32))
 
     far_z = zs // 2
-    cut = rows // 2
-    parts = {0: slice(0, cut), 1: slice(cut, rows)}
+    size = rows // PIECES
+    parts = [slice(i * size, (i + 1) * size) for i in range(PIECES)]
+    early = [list(range(PIECES // 2)), list(range(PIECES // 2, PIECES))]
     rs_copies = {}
 
-    def rs_copy(side, step, piece):
+    def rs_send(side, step, piece, have):
         way = 1 if side == 0 else -1
+        outgoing[side, step, parts[piece]] = have.astype(jnp.bfloat16)
         copy = pltpu.make_async_remote_copy(
             src_ref=outgoing.at[side, step, parts[piece]], dst_ref=incoming.at[side, step, parts[piece]],
-            send_sem=rs_send.at[side, step, piece], recv_sem=rs_recv.at[side, step, piece],
-            device_id=at_z(wrap(z + way, zs)), device_id_type=MESH)
+            send_sem=rs_out.at[side, step, piece], recv_sem=rs_in.at[side, step, piece],
+            device_id=to_z[way], device_id_type=MESH)
         rs_copies[side, step, piece] = copy
-        return copy
+        copy.start()
 
     value = partial_of(far_z)
-    for side in range(2):
-        outgoing[side, 0, parts[side]] = value[parts[side]].astype(jnp.bfloat16)
-        rs_copy(side, 0, side).start()
+    for i in range(PIECES // 2):
+        for side in range(2):
+            piece = early[side][i]
+            rs_send(side, 0, piece, value[parts[piece]])
     for step in range(1, far_z):
-        for side in range(2):
-            way = 1 if side == 0 else -1
-            value = partial_of(way * (far_z - step))
-            for piece in (1 - side, side):
-                have = value[parts[piece]]
-                if step > 1 or piece == side:
-                    rs_copies[side, step - 1, piece].wait_recv()
-                    have = have + incoming[side, step - 1, parts[piece]].astype(jnp.float32)
-                outgoing[side, step, parts[piece]] = have.astype(jnp.bfloat16)
-                rs_copy(side, step, piece).start()
+        values = [partial_of(far_z - step), partial_of(step - far_z)]
+        for piece_of in (early[::-1], early):
+            for i in range(PIECES // 2):
+                for side in range(2):
+                    piece = piece_of[side][i]
+                    have = values[side][parts[piece]]
+                    if (side, step - 1, piece) in rs_copies:
+                        rs_copies[side, step - 1, piece].wait_recv()
+                        have = have + incoming[side, step - 1, parts[piece]].astype(jnp.float32)
+                    rs_send(side, step, piece, have)
     value = partial_of(0)
-    for piece in range(2):
-        have = value[parts[piece]]
-        for side in range(2):
-            rs_copies[side, far_z - 1, piece].wait_recv()
-            have = have + incoming[side, far_z - 1, parts[piece]].astype(jnp.float32)
-        out_ref[parts[piece]] = have.astype(jnp.bfloat16)
+    for i in range(PIECES // 2):
+        for piece in (early[0][i], early[1][i]):
+            have = value[parts[piece]]
+            for side in range(2):
+                rs_copies[side, far_z - 1, piece].wait_recv()
+                have = have + incoming[side, far_z - 1, parts[piece]].astype(jnp.float32)
+            out_ref[parts[piece]] = have.astype(jnp.bfloat16)
 
     for copy in sends + wo_remote + state_copies + [swap_copy] + list(rs_copies.values()):
         copy.wait_send()
@@ -435,7 +447,7 @@
             pltpu.VMEM((2, far_z, rows, chans), b16),
             pltpu.VMEM((2, far_z, rows, chans), b16),
             dma((2 + zs,)), dma((moves,)), dma((moves,)), dma((zs,)), dma((zs,)), dma((2,)),
-            dma((2, n)), dma((2, n)), dma((2,)), dma((2, far_z, 2)), dma((2, far_z, 2)),
+            dma((2, n)), dma((2, n)), dma((2,)), dma((2, far_z, PIECES)), dma((2, far_z, PIECES)),
         ],
         compiler_params=pltpu.CompilerParams(
             collective_id=0, has_side_effects=True, vmem_limit_bytes=60 * 1024 * 1024),

time: 90.5 us -> 88.9 us (0.982)
  Pallas kernels: 88.8 us -> 87.2 us
    pallas_call x1, Pallas kernels: 88.8 us -> 87.2 us  [on_device(): pl.pallas_call(functools.partial(kernel, n, zs), out_shape=jax.ShapeDtype...]
where the time goes in v2:
time: 88.9 us; the launch traced here: 88.7 us
  Pallas kernels  87.2 us (98%)
  local copies, waits for them, and re-layouts  1.54 us (2%)
    pallas_call x1, Pallas kernels, on_device(): pl.pallas_call(functools.partial(kernel, n, zs), out_shape=jax.ShapeDtype...  87.2 us

profile of v2, /device:TPU:1, one launch (start us, length us, event | category | flops | bytes accessed | tf_op | source)
XLA Modules:
  0.0 88.7 jit_solution(2813620153428084549)
XLA Ops:
  0.0 87.2 %shard_map.64 = bf16[192,256]{1,0:T(8,128)(2,1)} custom-call(bf16[192,4096]{1,0:T(8,128)(2,1)} %tok_hbm.1, bf16[3,64,256]{2,1,0:T(8,128)(2,1)} %bitcast.1, f32[3,3,256]{2,1,0:T(4,128)} %taps_ref.1, f32[8,256]{1,0:T(8,128)} %decay_ref.1, f32[8,256]{1,0:T(8,128)} %residue_ref.1, bf16[256,4096]{1,0:T(8,128)(2,1)} %wo_hbm.1), custom_call_target="tpu_custom_call" | custom-call | tf_op jit(solution)/shard_map/pallas_call | solution.py:429
  87.2 1.5 %copy.8 = bf16[192,256]{1,0:T(8,128)(2,1)} copy(bf16[192,256]{1,0:T(8,128)(2,1)} %shard_map.64) | data formatting | bytes 196608
